TPU v7x, 32 devices: a whole 2x2x4 slice. The times are simulated.
32 devices in a mesh: groups: 2 (over y), seq: 8 (over z, x), chan: 2 (over core).
Axes of the slice: x: 2, y: 2, z: 4, core: 2. Of those that a mesh axis runs over, the one named last changes fastest.
Arguments:
- projected: bfloat16 [3, 2048, 1024], P(None, ('groups', 'seq'), 'chan'), parts along dimension 1, may hold values from -6 to 6
- long_filter: float32 [2048, 1024], P(('groups', 'seq'), 'chan'), parts along dimension 0, may hold values from -6 to 6
- short_kernel: float32 [3, 7, 1024], P(None, None, 'chan'), may hold values from -2 to 2
- skip_gain: float32 [1024], P('chan'), may hold values from 0.25 to 1.5
- cotangent: bfloat16 [2048, 1024], P(('groups', 'seq'), 'chan'), parts along dimension 0, may hold values from -6 to 6
Outputs:
- layer_output: bfloat16 [2048, 1024], P(('groups', 'seq'), 'chan'), parts along dimension 0
- stream_grads: bfloat16 [3, 2048, 1024], P(None, ('groups', 'seq'), 'chan'), parts along dimension 1
- filter_grad: float32 [2048, 1024], P(('groups', 'seq'), 'chan'), parts along dimension 0
- kernel_grad: float32 [6, 7, 1024], P('groups', None, 'chan'), parts along dimension 0
- skip_grad: float32 [2048], P(('groups', 'chan')), parts along dimension 0
There are 2 independent parts, one for each index of `groups`. A program takes and returns all parts, laid end to end along the dimension named above; an argument that names none is the same for every part. Nothing has to cross between parts.
All inputs are finite; a program needn't handle non-finite values.
Results may differ from a plain program's by a relative error of at most 0.001.
Values may be sent and summed in bfloat16 or wider, within the bound.
A program may use at most 64 MiB of HBM per device.

v0:
```python
import math
import jax
import jax.numpy as jnp
from jax import lax
from jax.sharding import PartitionSpec as P

HIGHEST = lax.Precision.HIGHEST


def with_halo(block, sides, width):
    for axis, dim in sides:
        count = lax.axis_size(axis)
        forward = [(i, i + 1) for i in range(count - 1)]
        forward.append((count - 1, 0))
        backward = [(target, source) for source, target in forward]
        low = lax.ppermute(
            lax.slice_in_dim(block, block.shape[dim] - width, None, axis=dim), axis, forward
        )
        high = lax.ppermute(lax.slice_in_dim(block, 0, width, axis=dim), axis, backward)
        block = jnp.concatenate([low, block, high], axis=dim)
    return block


def dft_tables(extent):
    indices = jnp.arange(extent, dtype=jnp.int32)
    angles = (indices[:, None] * indices[None, :] % extent).astype(jnp.float32) * (
        2.0 * math.pi / extent
    )
    return (jnp.cos(angles), jnp.sin(angles))


def apply_along(matrix, signal, axis_dim):
    letters = "wxyz"
    target = letters[:axis_dim] + "k" + letters[axis_dim + 1 :]
    return jnp.einsum(
        "k" + letters[axis_dim] + "," + letters + "->" + target, matrix, signal, precision=HIGHEST
    )


def forward_section(real_part, imaginary, axis_dim):
    cosine, sine_table = dft_tables(real_part.shape[axis_dim])
    out_real = apply_along(cosine, real_part, axis_dim)
    out_imag = -apply_along(sine_table, real_part, axis_dim)
    if imaginary is not None:
        out_real = out_real + apply_along(sine_table, imaginary, axis_dim)
        out_imag = out_imag + apply_along(cosine, imaginary, axis_dim)
    return (out_real, out_imag)


def inverse_section(real_part, imaginary, axis_dim, keep_imag):
    cosine, sine_table = dft_tables(real_part.shape[axis_dim])
    out_real = apply_along(cosine, real_part, axis_dim) - apply_along(
        sine_table, imaginary, axis_dim
    )
    if keep_imag:
        return (
            out_real,
            apply_along(sine_table, real_part, axis_dim) + apply_along(cosine, imaginary, axis_dim),
        )
    return (out_real, None)


def twist(real_part, imaginary, angles, sign_factor):
    cosine = jnp.cos(angles)
    sine_table = jnp.sin(angles)
    return (
        real_part * cosine + sign_factor * imaginary * sine_table,
        imaginary * cosine - sign_factor * real_part * sine_table,
    )


def twiddle(low_index, high_index, extent):
    return (low_index * high_index % extent).astype(jnp.float32) * (2.0 * math.pi / extent)


def block_angles(devices, portion, extent):
    low_index = jnp.arange(devices, dtype=jnp.int32)[None, :, None, None]
    high_index = (lax.axis_index("seq") * portion + jnp.arange(portion, dtype=jnp.int32))[
        None, None, :, None
    ]
    return twiddle(low_index, high_index, extent)


def sequence_forward(signals, extent):
    devices = lax.axis_size("seq")
    portion = signals.shape[1] // devices
    columns = lax.all_to_all(signals[:, None], "seq", split_axis=2, concat_axis=1, tiled=True)
    real_part, imaginary = forward_section(columns, None, 1)
    real_part, imaginary = twist(real_part, imaginary, block_angles(devices, portion, extent), 1.0)
    spread = (
        lax.all_to_all(real_part, "seq", split_axis=1, concat_axis=2, tiled=True),
        lax.all_to_all(imaginary, "seq", split_axis=1, concat_axis=2, tiled=True),
    )
    return forward_section(spread[0], spread[1], 2)


def sequence_inverse(real_part, imaginary, extent):
    devices = lax.axis_size("seq")
    portion = real_part.shape[2] // devices
    real_part, imaginary = inverse_section(real_part, imaginary, 2, True)
    gathered = (
        lax.all_to_all(real_part, "seq", split_axis=2, concat_axis=1, tiled=True),
        lax.all_to_all(imaginary, "seq", split_axis=2, concat_axis=1, tiled=True),
    )
    real_part, imaginary = twist(
        gathered[0], gathered[1], block_angles(devices, portion, extent), -1.0
    )
    pieces = inverse_section(real_part, imaginary, 1, False)[0] * (1.0 / extent)
    blocks = lax.all_to_all(pieces, "seq", split_axis=1, concat_axis=2, tiled=True)
    return blocks[:, 0]


def body(projected, long_filter, short_kernel, skip_gain, cotangent):
    rows_here = projected.shape[1]
    extent = rows_here * lax.axis_size("seq")
    factor = 1.0 / math.sqrt(extent)
    kernel_span = short_kernel.shape[1]
    margin = kernel_span // 2
    padded = with_halo(projected, (("seq", 1),), margin)
    shorts = jnp.zeros(projected.shape, jnp.float32)
    for offset in range(kernel_span):
        shorts = shorts + short_kernel[:, offset][:, None, :] * padded[
            :, offset : offset + rows_here
        ].astype(jnp.float32)
    gated_signal = shorts[1] * shorts[2]
    transform, restore = (sequence_forward, sequence_inverse)
    upstream = cotangent.astype(jnp.float32)
    grad_response = upstream * shorts[0]
    spec_real, spec_imag = transform(jnp.stack([gated_signal, long_filter]), extent)
    gated_real, gated_imag = (spec_real[0], spec_imag[0])
    filter_real, filter_imag = (spec_real[1] * factor, spec_imag[1] * factor)
    product_real = filter_real * gated_real - filter_imag * gated_imag
    product_imag = filter_real * gated_imag + filter_imag * gated_real
    convolved = restore(product_real[None], product_imag[None], extent)[0]
    upstream_real, upstream_imag = transform(grad_response[None], extent)
    upstream_real, upstream_imag = (upstream_real[0], upstream_imag[0])
    back_real = jnp.stack(
        [
            filter_real * upstream_real + filter_imag * upstream_imag,
            gated_real * upstream_real + gated_imag * upstream_imag,
        ]
    )
    back_imag = jnp.stack(
        [
            filter_real * upstream_imag - filter_imag * upstream_real,
            gated_real * upstream_imag - gated_imag * upstream_real,
        ]
    )
    restored = restore(back_real, back_imag, extent)
    grad_gated = restored[0] + skip_gain * grad_response
    filter_grad = restored[1] * factor
    response = convolved + skip_gain * gated_signal
    layer_output = (response * shorts[0]).astype(jnp.bfloat16)
    grad_shorts = jnp.stack([upstream * response, grad_gated * shorts[2], grad_gated * shorts[1]])
    rimmed = with_halo(grad_shorts, (("seq", 1),), margin)
    stream_sum = jnp.zeros(grad_shorts.shape, jnp.float32)
    kernel_terms = []
    for offset in range(kernel_span):
        start_row = 2 * margin - offset
        stream_sum = (
            stream_sum
            + short_kernel[:, offset][:, None, :] * rimmed[:, start_row : start_row + rows_here]
        )
        kernel_terms.append(
            jnp.sum(
                grad_shorts * padded[:, offset : offset + rows_here].astype(jnp.float32), axis=1
            )
        )
    kernel_part = jnp.stack(kernel_terms, axis=1)
    skip_part = jnp.sum(grad_response * gated_signal, axis=0)
    kernel_total, skip_total = lax.psum((kernel_part, skip_part), "seq")
    return (
        layer_output,
        stream_sum.astype(jnp.bfloat16),
        filter_grad,
        kernel_total * factor,
        skip_total * factor,
    )


def solution(mesh):
    placed = (
        P(None, ("groups", "seq"), "chan"),
        P(("groups", "seq"), "chan"),
        P(None, None, "chan"),
        P("chan"),
        P(("groups", "seq"), "chan"),
    )
    return jax.shard_map(
        body,
        mesh=mesh,
        in_specs=placed,
        out_specs=(
            P(("groups", "seq"), "chan"),
            P(None, ("groups", "seq"), "chan"),
            P(("groups", "seq"), "chan"),
            P("groups", None, "chan"),
            P(("groups", "chan")),
        ),
        check_vma=False,
    )
```

profile of v0, /device:TPU:0, one launch (start us, length us, event | category | flops | bytes accessed | tf_op | source)
XLA Modules:
  0.0 248.4 jit_solution(6842409723577557810)
XLA Ops:
  1.4 6.0 %collective-permute-start.1 = (bf16[3,3,512]{2,1,0:T(4,128)(2,1)S(1)}, bf16[3,3,512]{2,1,0:T(4,128)(2,1)S(1)}, u32[]{:S(2)}, u32[]{:S(2)}) collective-permute-start(bf16[3,3,512]{2,1,0:T(4,128)(2,1)S(1)} %get-tuple-element.52), channel_id=1, source_target_pairs={{2,0},{4,2},{6,4},{8,6},{10,8},{12,10},{14,12},{0,14},{3,1},{5,3},... | collective-permute-start | bytes 27656 | tf_op jit(solution)/shard_map/ppermute | solution.py:19
  8.9 5.0 %collective-permute-done = bf16[3,3,512]{2,1,0:T(4,128)(2,1)S(1)} collective-permute-done((bf16[3,3,512]{2,1,0:T(4,128)(2,1)S(1)}, bf16[3,3,512]{2,1,0:T(4,128)(2,1)S(1)}, u32[]{:S(2)}, u32[]{:S(2)}) %collective-permute-start) | collective-permute-done | bytes 9248 | tf_op jit(solution)/shard_map/ppermute | solution.py:16
  15.8 3.4 %all-to-all-start.6 = ((f32[1,1,128,512]{3,1,0,2:T(1,128)}), f32[1,1,128,512]{3,1,0,2:T(1,128)S(1)}, u32[]{:S(2)}, u32[]{:S(2)}) async-start(f32[1,1,128,512]{3,1,0,2:T(1,128)} %copy.61), calls=%async_computation.6 | async-start | bytes 524288 | tf_op jit(solution)/shard_map/all_to_all | solution.py:87
  21.4 6.0 %all-to-all-done.6 = f32[1,1,128,512]{3,1,0,2:T(1,128)S(1)} async-done(((f32[1,1,128,512]{3,1,0,2:T(1,128)}), f32[1,1,128,512]{3,1,0,2:T(1,128)S(1)}, u32[]{:S(2)}, u32[]{:S(2)}) %all-to-all-start.6) | async-done | bytes 262176 | tf_op jit(solution)/shard_map/all_to_all | solution.py:87
  27.3 3.5 %all-to-all-start = ((f32[2,1,128,512]{3,0,1,2:T(2,128)}), f32[2,1,128,512]{3,0,1,2:T(2,128)S(1)}, u32[]{:S(2)}, u32[]{:S(2)}) async-start(f32[2,1,128,512]{3,0,1,2:T(2,128)} %copy.42), calls=%async_computation | async-start | bytes 1048576 | tf_op jit(solution)/shard_map/all_to_all | solution.py:87
  33.0 10.4 %all-to-all-done = f32[2,1,128,512]{3,0,1,2:T(2,128)S(1)} async-done(((f32[2,1,128,512]{3,0,1,2:T(2,128)}), f32[2,1,128,512]{3,0,1,2:T(2,128)S(1)}, u32[]{:S(2)}, u32[]{:S(2)}) %all-to-all-start) | async-done | bytes 524320 | tf_op jit(solution)/shard_map/all_to_all | solution.py:87
  43.4 3.6 %all-to-all-start.7 = ((f32[1,8,16,512]{3,2,0,1:T(8,128)}), f32[1,8,16,512]{3,2,0,1:T(8,128)S(1)}, u32[]{:S(2)}, u32[]{:S(2)}) async-start(f32[1,8,16,512]{3,2,0,1:T(8,128)} %copy.64), calls=%async_computation.7 | async-start | bytes 524288 | tf_op jit(solution)/shard_map/all_to_all | solution.py:91
  48.0 7.3 %all-to-all-done.7 = f32[1,8,16,512]{3,2,0,1:T(8,128)S(1)} async-done(((f32[1,8,16,512]{3,2,0,1:T(8,128)}), f32[1,8,16,512]{3,2,0,1:T(8,128)S(1)}, u32[]{:S(2)}, u32[]{:S(2)}) %all-to-all-start.7) | async-done | bytes 262176 | tf_op jit(solution)/shard_map/all_to_all | solution.py:91
  55.3 3.4 %all-to-all-start.8 = ((f32[1,8,16,512]{3,2,0,1:T(8,128)}), f32[1,8,16,512]{3,2,0,1:T(8,128)S(1)}, u32[]{:S(2)}, u32[]{:S(2)}) async-start(f32[1,8,16,512]{3,2,0,1:T(8,128)} %copy.65), calls=%async_computation.8 | async-start | bytes 524288 | tf_op jit(solution)/shard_map/all_to_all | solution.py:92
  61.7 5.2 %all-to-all-done.8 = f32[1,8,16,512]{3,2,0,1:T(8,128)S(1)} async-done(((f32[1,8,16,512]{3,2,0,1:T(8,128)}), f32[1,8,16,512]{3,2,0,1:T(8,128)S(1)}, u32[]{:S(2)}, u32[]{:S(2)}) %all-to-all-start.8) | async-done | bytes 262176 | tf_op jit(solution)/shard_map/all_to_all | solution.py:92
  66.9 3.5 %all-to-all-start.2 = ((f32[2,8,16,512]{3,2,0,1:T(8,128)}), f32[2,8,16,512]{3,2,0,1:T(8,128)S(1)}, u32[]{:S(2)}, u32[]{:S(2)}) async-start(f32[2,8,16,512]{3,2,0,1:T(8,128)} %copy.49), calls=%async_computation.2 | async-start | bytes 1048576 | tf_op jit(solution)/shard_map/all_to_all | solution.py:92
  71.5 12.8 %all-to-all-done.2 = f32[2,8,16,512]{3,2,0,1:T(8,128)S(1)} async-done(((f32[2,8,16,512]{3,2,0,1:T(8,128)}), f32[2,8,16,512]{3,2,0,1:T(8,128)S(1)}, u32[]{:S(2)}, u32[]{:S(2)}) %all-to-all-start.2) | async-done | bytes 524320 | tf_op jit(solution)/shard_map/all_to_all | solution.py:92
  84.3 3.7 %all-to-all-start.1 = ((f32[2,8,16,512]{3,2,0,1:T(8,128)}), f32[2,8,16,512]{3,2,0,1:T(8,128)S(1)}, u32[]{:S(2)}, u32[]{:S(2)}) async-start(f32[2,8,16,512]{3,2,0,1:T(8,128)} %copy.46), calls=%async_computation.1 | async-start | bytes 1048576 | tf_op jit(solution)/shard_map/all_to_all | solution.py:91
  92.8 9.4 %all-to-all-done.1 = f32[2,8,16,512]{3,2,0,1:T(8,128)S(1)} async-done(((f32[2,8,16,512]{3,2,0,1:T(8,128)}), f32[2,8,16,512]{3,2,0,1:T(8,128)S(1)}, u32[]{:S(2)}, u32[]{:S(2)}) %all-to-all-start.1) | async-done | bytes 524320 | tf_op jit(solution)/shard_map/all_to_all | solution.py:91
  107.3 1.6 fusion.6
  108.9 2.0 copy.66
  111.0 4.1 %all-to-all-start.9 = ((f32[2,1,128,512]{3,0,1,2:T(2,128)}), f32[2,1,128,512]{3,0,1,2:T(2,128)}, u32[]{:S(2)}, u32[]{:S(2)}) async-start(f32[2,1,128,512]{3,0,1,2:T(2,128)} %copy.66), calls=%async_computation.9 | async-start | bytes 1048576 | tf_op jit(solution)/shard_map/all_to_all | solution.py:102
  117.8 11.4 %all-to-all-done.9 = f32[2,1,128,512]{3,0,1,2:T(2,128)} async-done(((f32[2,1,128,512]{3,0,1,2:T(2,128)}), f32[2,1,128,512]{3,0,1,2:T(2,128)}, u32[]{:S(2)}, u32[]{:S(2)}) %all-to-all-start.9) | async-done | bytes 524320 | tf_op jit(solution)/shard_map/all_to_all | solution.py:102
  129.2 3.7 %all-to-all-start.10 = ((f32[2,1,128,512]{3,0,1,2:T(2,128)}), f32[2,1,128,512]{3,0,1,2:T(2,128)S(1)}, u32[]{:S(2)}, u32[]{:S(2)}) async-start(f32[2,1,128,512]{3,0,1,2:T(2,128)} %copy.69), calls=%async_computation.10 | async-start | bytes 1048576 | tf_op jit(solution)/shard_map/all_to_all | solution.py:103
  135.0 12.2 %all-to-all-done.10 = f32[2,1,128,512]{3,0,1,2:T(2,128)S(1)} async-done(((f32[2,1,128,512]{3,0,1,2:T(2,128)}), f32[2,1,128,512]{3,0,1,2:T(2,128)S(1)}, u32[]{:S(2)}, u32[]{:S(2)}) %all-to-all-start.10) | async-done | bytes 524320 | tf_op jit(solution)/shard_map/all_to_all | solution.py:103
  147.2 3.6 %all-to-all-start.4 = ((f32[1,1,128,512]{3,1,0,2:T(1,128)}), f32[1,1,128,512]{3,1,0,2:T(1,128)S(1)}, u32[]{:S(2)}, u32[]{:S(2)}) async-start(f32[1,1,128,512]{3,1,0,2:T(1,128)} %copy.56), calls=%async_computation.4 | async-start | bytes 524288 | tf_op jit(solution)/shard_map/all_to_all | solution.py:103
  154.1 5.7 %all-to-all-done.4 = f32[1,1,128,512]{3,1,0,2:T(1,128)S(1)} async-done(((f32[1,1,128,512]{3,1,0,2:T(1,128)}), f32[1,1,128,512]{3,1,0,2:T(1,128)S(1)}, u32[]{:S(2)}, u32[]{:S(2)}) %all-to-all-start.4) | async-done | bytes 262176 | tf_op jit(solution)/shard_map/all_to_all | solution.py:103
  159.8 3.6 %all-to-all-start.3 = ((f32[1,1,128,512]{3,1,0,2:T(1,128)}), f32[1,1,128,512]{3,1,0,2:T(1,128)S(1)}, u32[]{:S(2)}, u32[]{:S(2)}) async-start(f32[1,1,128,512]{3,1,0,2:T(1,128)} %copy.54), calls=%async_computation.3 | async-start | bytes 524288 | tf_op jit(solution)/shard_map/all_to_all | solution.py:102
  166.9 5.1 %all-to-all-done.3 = f32[1,1,128,512]{3,1,0,2:T(1,128)S(1)} async-done(((f32[1,1,128,512]{3,1,0,2:T(1,128)}), f32[1,1,128,512]{3,1,0,2:T(1,128)S(1)}, u32[]{:S(2)}, u32[]{:S(2)}) %all-to-all-start.3) | async-done | bytes 262176 | tf_op jit(solution)/shard_map/all_to_all | solution.py:102
  172.0 3.6 %all-to-all-start.11 = ((f32[2,8,16,512]{3,2,0,1:T(8,128)}), f32[2,8,16,512]{3,2,0,1:T(8,128)S(1)}, u32[]{:S(2)}, u32[]{:S(2)}) async-start(f32[2,8,16,512]{3,2,0,1:T(8,128)} %copy.74), calls=%async_computation.11 | async-start | bytes 1048576 | tf_op jit(solution)/shard_map/all_to_all | solution.py:109
  177.8 11.8 %all-to-all-done.11 = f32[2,8,16,512]{3,2,0,1:T(8,128)S(1)} async-done(((f32[2,8,16,512]{3,2,0,1:T(8,128)}), f32[2,8,16,512]{3,2,0,1:T(8,128)S(1)}, u32[]{:S(2)}, u32[]{:S(2)}) %all-to-all-start.11) | async-done | bytes 524320 | tf_op jit(solution)/shard_map/all_to_all | solution.py:109
  189.6 3.6 %all-to-all-start.5 = ((f32[1,8,16,512]{3,2,0,1:T(8,128)}), f32[1,8,16,512]{3,2,0,1:T(8,128)S(1)}, u32[]{:S(2)}, u32[]{:S(2)}) async-start(f32[1,8,16,512]{3,2,0,1:T(8,128)} %copy.60), calls=%async_computation.5 | async-start | bytes 524288 | tf_op jit(solution)/shard_map/all_to_all | solution.py:109
  193.3 8.6 %all-to-all-done.5 = f32[1,8,16,512]{3,2,0,1:T(8,128)S(1)} async-done(((f32[1,8,16,512]{3,2,0,1:T(8,128)}), f32[1,8,16,512]{3,2,0,1:T(8,128)S(1)}, u32[]{:S(2)}, u32[]{:S(2)}) %all-to-all-start.5) | async-done | bytes 262176 | tf_op jit(solution)/shard_map/all_to_all | solution.py:109
  201.9 1.7 fusion.52
  204.5 35.7 %all-reduce = (f32[3,7,512]{2,0,1:T(4,128)S(1)}, f32[512]{0:T(512)S(1)}) all-reduce(f32[3,7,512]{2,0,1:T(4,128)S(1)} %constant_dynamic-update-slice_fusion.2, f32[512]{0:T(512)S(1)} %get-tuple-element.38), channel_id=1, replica_groups=mesh['groups'=2,'seq'=8,'chan'=2] {'seq'}, use_global_device_ids=true, to_apply=%region_7.8 | all-reduce | flops 11264 | bytes 90112 | tf_op jit(solution)/shard_map/psum | solution.py:171
  240.4 2.0 collective-permute-start.3
  244.3 2.6 %collective-permute-done.3 = f32[3,3,512]{2,1,0:T(4,128)S(1)} collective-permute-done((f32[3,3,512]{2,1,0:T(4,128)S(1)}, f32[3,3,512]{2,1,0:T(4,128)S(1)}, u32[]{:S(2)}, u32[]{:S(2)}) %collective-permute-start.3) | collective-permute-done | bytes 18464 | tf_op jit(solution)/shard_map/ppermute | solution.py:16
  (93 shorter events, 41.3 us)
Async XLA Ops:
  0.6 6.8 %copy-start.5 = (f32[3,7,512]{2,1,0:T(8,128)S(1)}, f32[3,7,512]{2,1,0:T(8,128)}, u32[]{:S(2)}) copy-start(f32[3,7,512]{2,1,0:T(8,128)} %param.7) | copy-start | bytes 129028
  1.4 7.4 %collective-permute-start.1 = (bf16[3,3,512]{2,1,0:T(4,128)(2,1)S(1)}, bf16[3,3,512]{2,1,0:T(4,128)(2,1)S(1)}, u32[]{:S(2)}, u32[]{:S(2)}) collective-permute-start(bf16[3,3,512]{2,1,0:T(4,128)(2,1)S(1)} %get-tuple-element.52), channel_id=1, source_target_pairs={{2,0},{4,2},{6,4},{8,6},{10,8},{12,10},{14,12},{0,14},{3,1},{5,3},... | collective-permute-start | bytes 27656 | tf_op jit(solution)/shard_map/ppermute | solution.py:19
  7.5 6.4 %collective-permute-start = (bf16[3,3,512]{2,1,0:T(4,128)(2,1)S(1)}, bf16[3,3,512]{2,1,0:T(4,128)(2,1)S(1)}, u32[]{:S(2)}, u32[]{:S(2)}) collective-permute-start(bf16[3,3,512]{2,1,0:T(4,128)(2,1)S(1)} %get-tuple-element.53), channel_id=1, source_target_pairs={{0,2},{2,4},{4,6},{6,8},{8,10},{10,12},{12,14},{14,0},{1,3},{3,5},... | collective-permute-start | bytes 27656 | tf_op jit(solution)/shard_map/ppermute | solution.py:16
  7.5 6.3 %copy-start = (bf16[3,128,512]{2,1,0:T(8,128)(2,1)S(1)}, bf16[3,128,512]{2,1,0:T(8,128)(2,1)}, u32[]{:S(2)}) copy-start(bf16[3,128,512]{2,1,0:T(8,128)(2,1)} %param.5) | copy-start | bytes 1179652
  13.8 0.9 copy-start.3
  15.8 11.6 %all-to-all-start.6 = ((f32[1,1,128,512]{3,1,0,2:T(1,128)}), f32[1,1,128,512]{3,1,0,2:T(1,128)S(1)}, u32[]{:S(2)}, u32[]{:S(2)}) async-start(f32[1,1,128,512]{3,1,0,2:T(1,128)} %copy.61), calls=%async_computation.6 | async-start | bytes 524288 | tf_op jit(solution)/shard_map/all_to_all | solution.py:87
  19.2 1.0 copy-start.4
  27.3 16.0 %all-to-all-start = ((f32[2,1,128,512]{3,0,1,2:T(2,128)}), f32[2,1,128,512]{3,0,1,2:T(2,128)S(1)}, u32[]{:S(2)}, u32[]{:S(2)}) async-start(f32[2,1,128,512]{3,0,1,2:T(2,128)} %copy.42), calls=%async_computation | async-start | bytes 1048576 | tf_op jit(solution)/shard_map/all_to_all | solution.py:87
  43.4 11.9 %all-to-all-start.7 = ((f32[1,8,16,512]{3,2,0,1:T(8,128)}), f32[1,8,16,512]{3,2,0,1:T(8,128)S(1)}, u32[]{:S(2)}, u32[]{:S(2)}) async-start(f32[1,8,16,512]{3,2,0,1:T(8,128)} %copy.64), calls=%async_computation.7 | async-start | bytes 524288 | tf_op jit(solution)/shard_map/all_to_all | solution.py:91
  55.3 11.6 %all-to-all-start.8 = ((f32[1,8,16,512]{3,2,0,1:T(8,128)}), f32[1,8,16,512]{3,2,0,1:T(8,128)S(1)}, u32[]{:S(2)}, u32[]{:S(2)}) async-start(f32[1,8,16,512]{3,2,0,1:T(8,128)} %copy.65), calls=%async_computation.8 | async-start | bytes 524288 | tf_op jit(solution)/shard_map/all_to_all | solution.py:92
  66.9 17.4 %all-to-all-start.2 = ((f32[2,8,16,512]{3,2,0,1:T(8,128)}), f32[2,8,16,512]{3,2,0,1:T(8,128)S(1)}, u32[]{:S(2)}, u32[]{:S(2)}) async-start(f32[2,8,16,512]{3,2,0,1:T(8,128)} %copy.49), calls=%async_computation.2 | async-start | bytes 1048576 | tf_op jit(solution)/shard_map/all_to_all | solution.py:92
  84.3 17.9 %all-to-all-start.1 = ((f32[2,8,16,512]{3,2,0,1:T(8,128)}), f32[2,8,16,512]{3,2,0,1:T(8,128)S(1)}, u32[]{:S(2)}, u32[]{:S(2)}) async-start(f32[2,8,16,512]{3,2,0,1:T(8,128)} %copy.46), calls=%async_computation.1 | async-start | bytes 1048576 | tf_op jit(solution)/shard_map/all_to_all | solution.py:91
  104.5 1.2 copy-start.1
  104.5 1.2 copy-start.2
  111.0 18.2 %all-to-all-start.9 = ((f32[2,1,128,512]{3,0,1,2:T(2,128)}), f32[2,1,128,512]{3,0,1,2:T(2,128)}, u32[]{:S(2)}, u32[]{:S(2)}) async-start(f32[2,1,128,512]{3,0,1,2:T(2,128)} %copy.66), calls=%async_computation.9 | async-start | bytes 1048576 | tf_op jit(solution)/shard_map/all_to_all | solution.py:102
  129.2 18.0 %all-to-all-start.10 = ((f32[2,1,128,512]{3,0,1,2:T(2,128)}), f32[2,1,128,512]{3,0,1,2:T(2,128)S(1)}, u32[]{:S(2)}, u32[]{:S(2)}) async-start(f32[2,1,128,512]{3,0,1,2:T(2,128)} %copy.69), calls=%async_computation.10 | async-start | bytes 1048576 | tf_op jit(solution)/shard_map/all_to_all | solution.py:103
  147.2 12.6 %all-to-all-start.4 = ((f32[1,1,128,512]{3,1,0,2:T(1,128)}), f32[1,1,128,512]{3,1,0,2:T(1,128)S(1)}, u32[]{:S(2)}, u32[]{:S(2)}) async-start(f32[1,1,128,512]{3,1,0,2:T(1,128)} %copy.56), calls=%async_computation.4 | async-start | bytes 524288 | tf_op jit(solution)/shard_map/all_to_all | solution.py:103
  159.8 12.2 %all-to-all-start.3 = ((f32[1,1,128,512]{3,1,0,2:T(1,128)}), f32[1,1,128,512]{3,1,0,2:T(1,128)S(1)}, u32[]{:S(2)}, u32[]{:S(2)}) async-start(f32[1,1,128,512]{3,1,0,2:T(1,128)} %copy.54), calls=%async_computation.3 | async-start | bytes 524288 | tf_op jit(solution)/shard_map/all_to_all | solution.py:102
  172.0 17.6 %all-to-all-start.11 = ((f32[2,8,16,512]{3,2,0,1:T(8,128)}), f32[2,8,16,512]{3,2,0,1:T(8,128)S(1)}, u32[]{:S(2)}, u32[]{:S(2)}) async-start(f32[2,8,16,512]{3,2,0,1:T(8,128)} %copy.74), calls=%async_computation.11 | async-start | bytes 1048576 | tf_op jit(solution)/shard_map/all_to_all | solution.py:109
  189.6 12.3 %all-to-all-start.5 = ((f32[1,8,16,512]{3,2,0,1:T(8,128)}), f32[1,8,16,512]{3,2,0,1:T(8,128)S(1)}, u32[]{:S(2)}, u32[]{:S(2)}) async-start(f32[1,8,16,512]{3,2,0,1:T(8,128)} %copy.60), calls=%async_computation.5 | async-start | bytes 524288 | tf_op jit(solution)/shard_map/all_to_all | solution.py:109
  193.2 8.7 %copy-start.6 = (f32[512]{0:T(512)S(1)}, f32[512]{0:T(512)}, u32[]{:S(2)}) copy-start(f32[512]{0:T(512)} %param.8) | copy-start | bytes 6148
  240.3 4.0 %collective-permute-start.2 = (f32[3,3,512]{2,1,0:T(4,128)S(1)}, f32[3,3,512]{2,1,0:T(4,128)S(1)}, u32[]{:S(2)}, u32[]{:S(2)}) collective-permute-start(f32[3,3,512]{2,1,0:T(4,128)S(1)} %get-tuple-element.46), channel_id=1, source_target_pairs={{2,0},{4,2},{6,4},{8,6},{10,8},{12,10},{14,12},{0,14},{3,1},{5,3},... | collective-permute-start | bytes 55304 | tf_op jit(solution)/shard_map/ppermute | solution.py:19
  240.4 6.6 %collective-permute-start.3 = (f32[3,3,512]{2,1,0:T(4,128)S(1)}, f32[3,3,512]{2,1,0:T(4,128)S(1)}, u32[]{:S(2)}, u32[]{:S(2)}) collective-permute-start(f32[3,3,512]{2,1,0:T(4,128)S(1)} %get-tuple-element.47), channel_id=1, source_target_pairs={{0,2},{2,4},{4,6},{6,8},{8,10},{10,12},{12,14},{14,0},{1,3},{3,5},... | collective-permute-start | bytes 55304 | tf_op jit(solution)/shard_map/ppermute | solution.py:16
where the time goes:
time: 250 us; the launch traced here: 248 us
  waiting for transfers between devices  114 us (46%)
  starting transfers between devices  51.5 us (21%)
  blocking collectives  35.7 us (14%)
  matrix products  21.8 us (9%)
  local copies, waits for them, and re-layouts  18.2 us (7%)
  other arithmetic  6.43 us (3%)
    psum x1, blocking collectives, body(): kernel_total, skip_total = lax.psum((kernel_part, skip_part), 'seq')  35.7 us
    dot_general x24, matrix products, apply_along(): jnp.einsum('k' + letters[axis_dim] + ',' + letters + '->' + target, matri...  21.8 us
    all_to_all x2, waiting for transfers between devices, sequence_inverse(): lax.all_to_all(pieces, 'seq', split_axis=1, concat_axis=2, tiled=True)  20.5 us
    all_to_all x2, waiting for transfers between devices, sequence_forward(): lax.all_to_all(imaginary, 'seq', split_axis=1, concat_axis=2, tiled=True)  18 us
    all_to_all x2, waiting for transfers between devices, sequence_inverse(): lax.all_to_all(imaginary, 'seq', split_axis=2, concat_axis=1, tiled=True)  17.8 us
    all_to_all x2, waiting for transfers between devices, sequence_forward(): lax.all_to_all(real_part, 'seq', split_axis=1, concat_axis=2, tiled=True)  16.7 us
    all_to_all x2, waiting for transfers between devices, sequence_inverse(): lax.all_to_all(real_part, 'seq', split_axis=2, concat_axis=1, tiled=True)  16.5 us
    all_to_all x2, waiting for transfers between devices, sequence_forward(): lax.all_to_all(signals[:, None], 'seq', split_axis=2, concat_axis=1, tile...  16.4 us
  transfers between devices with their start and end apart: 16, of which 15 were waited for; matrix products, arithmetic and copies ran while one was open for 12% of the time, Pallas kernels for 0%

commit v1 on v0

--- a/solution.py
+++ b/solution.py
@@ -5,6 +5,22 @@
 from jax.sharding import PartitionSpec as P
 
 HIGHEST = lax.Precision.HIGHEST
+
+
+def exchange_in_pairs(array, axis, split, join):
+    ways, here = (lax.axis_size(axis), lax.axis_index(axis))
+    width = array.shape[split] // ways
+    dims = list(array.shape)
+    dims[split] = width
+    height = dims[join]
+    dims[join] = height * ways
+    full = jnp.zeros(dims, array.dtype)
+    for mask in range(ways):
+        part = lax.dynamic_slice_in_dim(array, (here ^ mask) * width, width, axis=split)
+        if mask:
+            part = lax.ppermute(part, axis, [(d, d ^ mask) for d in range(ways)])
+        full = lax.dynamic_update_slice_in_dim(full, part, (here ^ mask) * height, axis=join)
+    return full
 
 
 def with_halo(block, sides, width):
@@ -99,7 +115,7 @@
     portion = real_part.shape[2] // devices
     real_part, imaginary = inverse_section(real_part, imaginary, 2, True)
     gathered = (
-        lax.all_to_all(real_part, "seq", split_axis=2, concat_axis=1, tiled=True),
+        exchange_in_pairs(real_part, "seq", 2, 1),
         lax.all_to_all(imaginary, "seq", split_axis=2, concat_axis=1, tiled=True),
     )
     real_part, imaginary = twist(

time: 250 us -> 238 us (0.952)
  waiting for transfers between devices: 114 us -> 80.2 us
  starting transfers between devices: 51.5 us -> 67.2 us
  local copies, waits for them, and re-layouts: 18.2 us -> 25 us
    ppermute x0 -> x14, starting transfers between devices: none -> 21.4 us  [exchange_in_pairs(): part = lax.ppermute(part, axis, [(d, d ^ mask) for d in range(ways)])]
    all_to_all x2 -> x0, waiting for transfers between devices: 16.5 us -> none  [sequence_inverse(): lax.all_to_all(real_part, 'seq', split_axis=2, concat_axis=1, tiled=True)]
    all_to_all x2, waiting for transfers between devices: 17.8 us -> 4.07 us  [sequence_inverse(): lax.all_to_all(imaginary, 'seq', split_axis=2, concat_axis=1, tiled=True)]
    all_to_all x2, waiting for transfers between devices: 20.5 us -> 7.86 us  [sequence_inverse(): lax.all_to_all(pieces, 'seq', split_axis=1, concat_axis=2, tiled=True)]
    ppermute x0 -> x14, waiting for transfers between devices: none -> 9.06 us  [exchange_in_pairs(): part = lax.ppermute(part, axis, [(d, d ^ mask) for d in range(ways)])]
    all_to_all x2 -> x0, starting transfers between devices: 7.73 us -> none  [sequence_inverse(): lax.all_to_all(real_part, 'seq', split_axis=2, concat_axis=1, tiled=True)]
    dynamic_update_slice x0 -> x16, local copies, waits for them, and re-layouts: none -> 6.28 us  [exchange_in_pairs(): lax.dynamic_update_slice_in_dim(full, part, (here ^ mask) * height, axis=...]
    sub x2 -> x0, local copies, waits for them, and re-layouts: 2.87 us -> none  [inverse_section(): apply_along(cosine, real_part, axis_dim)]
  transfers between devices with their start and end apart: 16 -> 28, of which waited for: 15 -> 15; matrix products, arithmetic and copies ran while one was open for 12% -> 14% of each run, Pallas kernels for 0% -> 0%
where the time goes in v1:
time: 238 us; the launch traced here: 237 us
  waiting for transfers between devices  80.2 us (34%)
  starting transfers between devices  67.2 us (28%)
  blocking collectives  34.9 us (15%)
  local copies, waits for them, and re-layouts  25 us (11%)
  matrix products  21.6 us (9%)
  other arithmetic  6.3 us (3%)
    psum x1, blocking collectives, body(): kernel_total, skip_total = lax.psum((kernel_part, skip_part), 'seq')  34.9 us
    dot_general x24, matrix products, apply_along(): jnp.einsum('k' + letters[axis_dim] + ',' + letters + '->' + target, matri...  21.6 us
    ppermute x14, starting transfers between devices, exchange_in_pairs(): part = lax.ppermute(part, axis, [(d, d ^ mask) for d in range(ways)])  21.4 us
    all_to_all x2, waiting for transfers between devices, sequence_forward(): lax.all_to_all(imaginary, 'seq', split_axis=1, concat_axis=2, tiled=True)  18 us
    all_to_all x2, waiting for transfers between devices, sequence_forward(): lax.all_to_all(real_part, 'seq', split_axis=1, concat_axis=2, tiled=True)  16.6 us
    all_to_all x2, waiting for transfers between devices, sequence_forward(): lax.all_to_all(signals[:, None], 'seq', split_axis=2, concat_axis=1, tile...  16.4 us
    all_to_all x2, starting transfers between devices, sequence_inverse(): lax.all_to_all(imaginary, 'seq', split_axis=2, concat_axis=1, tiled=True)  9.34 us
    ppermute x14, waiting for transfers between devices, exchange_in_pairs(): part = lax.ppermute(part, axis, [(d, d ^ mask) for d in range(ways)])  9.06 us
  transfers between devices with their start and end apart: 28, of which 15 were waited for; matrix products, arithmetic and copies ran while one was open for 14% of the time, Pallas kernels for 0%

profile of v1, /device:TPU:0, one launch (start us, length us, event | category | flops | bytes accessed | tf_op | source)
XLA Modules:
  0.0 236.7 jit_solution(6122357659631129663)
XLA Ops:
  1.4 6.0 %collective-permute-start.1 = (bf16[3,3,512]{2,1,0:T(4,128)(2,1)S(1)}, bf16[3,3,512]{2,1,0:T(4,128)(2,1)S(1)}, u32[]{:S(2)}, u32[]{:S(2)}) collective-permute-start(bf16[3,3,512]{2,1,0:T(4,128)(2,1)S(1)} %get-tuple-element.58), channel_id=1, source_target_pairs={{2,0},{4,2},{6,4},{8,6},{10,8},{12,10},{14,12},{0,14},{3,1},{5,3},... | collective-permute-start | bytes 27656 | tf_op jit(solution)/shard_map/ppermute | solution.py:35
  8.9 5.0 %collective-permute-done = bf16[3,3,512]{2,1,0:T(4,128)(2,1)S(1)} collective-permute-done((bf16[3,3,512]{2,1,0:T(4,128)(2,1)S(1)}, bf16[3,3,512]{2,1,0:T(4,128)(2,1)S(1)}, u32[]{:S(2)}, u32[]{:S(2)}) %collective-permute-start) | collective-permute-done | bytes 9248 | tf_op jit(solution)/shard_map/ppermute | solution.py:32
  15.8 3.4 %all-to-all-start.5 = ((f32[1,1,128,512]{3,1,0,2:T(1,128)}), f32[1,1,128,512]{3,1,0,2:T(1,128)S(1)}, u32[]{:S(2)}, u32[]{:S(2)}) async-start(f32[1,1,128,512]{3,1,0,2:T(1,128)} %copy.54), calls=%async_computation.5 | async-start | bytes 524288 | tf_op jit(solution)/shard_map/all_to_all | solution.py:103
  21.4 6.0 %all-to-all-done.5 = f32[1,1,128,512]{3,1,0,2:T(1,128)S(1)} async-done(((f32[1,1,128,512]{3,1,0,2:T(1,128)}), f32[1,1,128,512]{3,1,0,2:T(1,128)S(1)}, u32[]{:S(2)}, u32[]{:S(2)}) %all-to-all-start.5) | async-done | bytes 262176 | tf_op jit(solution)/shard_map/all_to_all | solution.py:103
  27.3 3.5 %all-to-all-start = ((f32[2,1,128,512]{3,0,1,2:T(2,128)}), f32[2,1,128,512]{3,0,1,2:T(2,128)S(1)}, u32[]{:S(2)}, u32[]{:S(2)}) async-start(f32[2,1,128,512]{3,0,1,2:T(2,128)} %copy.38), calls=%async_computation | async-start | bytes 1048576 | tf_op jit(solution)/shard_map/all_to_all | solution.py:103
  33.0 10.4 %all-to-all-done = f32[2,1,128,512]{3,0,1,2:T(2,128)S(1)} async-done(((f32[2,1,128,512]{3,0,1,2:T(2,128)}), f32[2,1,128,512]{3,0,1,2:T(2,128)S(1)}, u32[]{:S(2)}, u32[]{:S(2)}) %all-to-all-start) | async-done | bytes 524320 | tf_op jit(solution)/shard_map/all_to_all | solution.py:103
  43.4 3.6 %all-to-all-start.6 = ((f32[1,8,16,512]{3,2,0,1:T(8,128)}), f32[1,8,16,512]{3,2,0,1:T(8,128)S(1)}, u32[]{:S(2)}, u32[]{:S(2)}) async-start(f32[1,8,16,512]{3,2,0,1:T(8,128)} %copy.57), calls=%async_computation.6 | async-start | bytes 524288 | tf_op jit(solution)/shard_map/all_to_all | solution.py:107
  48.0 7.3 %all-to-all-done.6 = f32[1,8,16,512]{3,2,0,1:T(8,128)S(1)} async-done(((f32[1,8,16,512]{3,2,0,1:T(8,128)}), f32[1,8,16,512]{3,2,0,1:T(8,128)S(1)}, u32[]{:S(2)}, u32[]{:S(2)}) %all-to-all-start.6) | async-done | bytes 262176 | tf_op jit(solution)/shard_map/all_to_all | solution.py:107
  55.3 3.4 %all-to-all-start.7 = ((f32[1,8,16,512]{3,2,0,1:T(8,128)}), f32[1,8,16,512]{3,2,0,1:T(8,128)S(1)}, u32[]{:S(2)}, u32[]{:S(2)}) async-start(f32[1,8,16,512]{3,2,0,1:T(8,128)} %copy.58), calls=%async_computation.7 | async-start | bytes 524288 | tf_op jit(solution)/shard_map/all_to_all | solution.py:108
  61.7 5.2 %all-to-all-done.7 = f32[1,8,16,512]{3,2,0,1:T(8,128)S(1)} async-done(((f32[1,8,16,512]{3,2,0,1:T(8,128)}), f32[1,8,16,512]{3,2,0,1:T(8,128)S(1)}, u32[]{:S(2)}, u32[]{:S(2)}) %all-to-all-start.7) | async-done | bytes 262176 | tf_op jit(solution)/shard_map/all_to_all | solution.py:108
  66.9 3.5 %all-to-all-start.2 = ((f32[2,8,16,512]{3,2,0,1:T(8,128)}), f32[2,8,16,512]{3,2,0,1:T(8,128)S(1)}, u32[]{:S(2)}, u32[]{:S(2)}) async-start(f32[2,8,16,512]{3,2,0,1:T(8,128)} %copy.45), calls=%async_computation.2 | async-start | bytes 1048576 | tf_op jit(solution)/shard_map/all_to_all | solution.py:108
  71.5 12.8 %all-to-all-done.2 = f32[2,8,16,512]{3,2,0,1:T(8,128)S(1)} async-done(((f32[2,8,16,512]{3,2,0,1:T(8,128)}), f32[2,8,16,512]{3,2,0,1:T(8,128)S(1)}, u32[]{:S(2)}, u32[]{:S(2)}) %all-to-all-start.2) | async-done | bytes 524320 | tf_op jit(solution)/shard_map/all_to_all | solution.py:108
  84.3 3.7 %all-to-all-start.1 = ((f32[2,8,16,512]{3,2,0,1:T(8,128)}), f32[2,8,16,512]{3,2,0,1:T(8,128)S(1)}, u32[]{:S(2)}, u32[]{:S(2)}) async-start(f32[2,8,16,512]{3,2,0,1:T(8,128)} %copy.42), calls=%async_computation.1 | async-start | bytes 1048576 | tf_op jit(solution)/shard_map/all_to_all | solution.py:107
  92.8 9.3 %all-to-all-done.1 = f32[2,8,16,512]{3,2,0,1:T(8,128)S(1)} async-done(((f32[2,8,16,512]{3,2,0,1:T(8,128)}), f32[2,8,16,512]{3,2,0,1:T(8,128)S(1)}, u32[]{:S(2)}, u32[]{:S(2)}) %all-to-all-start.1) | async-done | bytes 524320 | tf_op jit(solution)/shard_map/all_to_all | solution.py:107
  111.1 2.0 copy.61
  113.1 4.4 %all-to-all-start.8 = ((f32[2,1,128,512]{3,0,1,2:T(2,128)}), f32[2,1,128,512]{3,0,1,2:T(2,128)}, u32[]{:S(2)}, u32[]{:S(2)}) async-start(f32[2,1,128,512]{3,0,1,2:T(2,128)} %copy.61), calls=%async_computation.8 | async-start | bytes 1048576 | tf_op jit(solution)/shard_map/all_to_all | solution.py:119
  119.2 1.7 collective-permute-start.9
  124.1 2.7 %collective-permute-start.12 = (f32[2,1,16,512]{3,1,2,0:T(1,128)S(1)}, f32[2,1,16,512]{3,1,2,0:T(1,128)S(1)}, u32[]{:S(2)}, u32[]{:S(2)}) collective-permute-start(f32[2,1,16,512]{3,1,2,0:T(1,128)S(1)} %reshape_bitcast_fusion.3), channel_id=1, source_target_pairs={{0,8},{2,10},{4,12},{6,14},{8,0},{10,2},{12,4},{14,6},{1,9},{3,11}... | collective-permute-start | bytes 196616 | tf_op jit(solution)/shard_map/ppermute | solution.py:21
  131.2 3.4 %collective-permute-start.14 = (f32[2,1,16,512]{3,1,2,0:T(1,128)S(1)}, f32[2,1,16,512]{3,1,2,0:T(1,128)S(1)}, u32[]{:S(2)}, u32[]{:S(2)}) collective-permute-start(f32[2,1,16,512]{3,1,2,0:T(1,128)S(1)} %reshape_bitcast_fusion.1), channel_id=1, source_target_pairs={{0,12},{2,14},{4,8},{6,10},{8,4},{10,6},{12,0},{14,2},{1,13},{3,15... | collective-permute-start | bytes 196616 | tf_op jit(solution)/shard_map/ppermute | solution.py:21
  136.8 1.7 collective-permute-start.2
  139.9 1.9 collective-permute-done.13
  144.0 5.0 %all-to-all-start.3 = ((f32[1,1,128,512]{3,1,0,2:T(1,128)}), f32[1,1,128,512]{3,1,0,2:T(1,128)S(1)}, u32[]{:S(2)}, u32[]{:S(2)}) async-start(f32[1,1,128,512]{3,1,0,2:T(1,128)} %copy.50), calls=%async_computation.3 | async-start | bytes 524288 | tf_op jit(solution)/shard_map/all_to_all | solution.py:119
  153.1 4.1 %all-to-all-done.3 = f32[1,1,128,512]{3,1,0,2:T(1,128)S(1)} async-done(((f32[1,1,128,512]{3,1,0,2:T(1,128)}), f32[1,1,128,512]{3,1,0,2:T(1,128)S(1)}, u32[]{:S(2)}, u32[]{:S(2)}) %all-to-all-start.3) | async-done | bytes 262176 | tf_op jit(solution)/shard_map/all_to_all | solution.py:119
  157.2 3.5 %all-to-all-start.9 = ((f32[2,8,16,512]{3,2,0,1:T(8,128)}), f32[2,8,16,512]{3,2,0,1:T(8,128)S(1)}, u32[]{:S(2)}, u32[]{:S(2)}) async-start(f32[2,8,16,512]{3,2,0,1:T(8,128)} %copy.65), calls=%async_computation.9 | async-start | bytes 1048576 | tf_op jit(solution)/shard_map/all_to_all | solution.py:125
  160.7 2.9 %collective-permute-start.5 = (f32[1,1,16,512]{3,1,2,0:T(1,128)S(1)}, f32[1,1,16,512]{3,1,2,0:T(1,128)S(1)}, u32[]{:S(2)}, u32[]{:S(2)}) collective-permute-start(f32[1,1,16,512]{3,1,2,0:T(1,128)S(1)} %reshape_bitcast_fusion.11), channel_id=1, source_target_pairs={{0,8},{2,10},{4,12},{6,14},{8,0},{10,2},{12,4},{14,6},{1,9},{3,11}... | collective-permute-start | bytes 98312 | tf_op jit(solution)/shard_map/ppermute | solution.py:21
  165.2 3.4 %collective-permute-start.7 = (f32[1,1,16,512]{3,1,2,0:T(1,128)S(1)}, f32[1,1,16,512]{3,1,2,0:T(1,128)S(1)}, u32[]{:S(2)}, u32[]{:S(2)}) collective-permute-start(f32[1,1,16,512]{3,1,2,0:T(1,128)S(1)} %reshape_bitcast_fusion.9), channel_id=1, source_target_pairs={{0,12},{2,14},{4,8},{6,10},{8,4},{10,6},{12,0},{14,2},{1,13},{3,15... | collective-permute-start | bytes 98312 | tf_op jit(solution)/shard_map/ppermute | solution.py:21
  169.4 5.8 %collective-permute-done.5 = f32[1,1,16,512]{3,1,2,0:T(1,128)S(1)} collective-permute-done((f32[1,1,16,512]{3,1,2,0:T(1,128)S(1)}, f32[1,1,16,512]{3,1,2,0:T(1,128)S(1)}, u32[]{:S(2)}, u32[]{:S(2)}) %collective-permute-start.5) | collective-permute-done | bytes 32800 | tf_op jit(solution)/shard_map/ppermute | solution.py:21
  178.9 3.7 %all-to-all-start.4 = ((f32[1,8,16,512]{3,2,0,1:T(8,128)}), f32[1,8,16,512]{3,2,0,1:T(8,128)S(1)}, u32[]{:S(2)}, u32[]{:S(2)}) async-start(f32[1,8,16,512]{3,2,0,1:T(8,128)} %copy.53), calls=%async_computation.4 | async-start | bytes 524288 | tf_op jit(solution)/shard_map/all_to_all | solution.py:125
  182.6 7.9 %all-to-all-done.4 = f32[1,8,16,512]{3,2,0,1:T(8,128)S(1)} async-done(((f32[1,8,16,512]{3,2,0,1:T(8,128)}), f32[1,8,16,512]{3,2,0,1:T(8,128)S(1)}, u32[]{:S(2)}, u32[]{:S(2)}) %all-to-all-start.4) | async-done | bytes 262176 | tf_op jit(solution)/shard_map/all_to_all | solution.py:125
  190.5 1.7 fusion.48
  193.1 34.9 %all-reduce = (f32[3,7,512]{2,0,1:T(4,128)S(1)}, f32[512]{0:T(512)S(1)}) all-reduce(f32[3,7,512]{2,0,1:T(4,128)S(1)} %constant_dynamic-update-slice_fusion.2, f32[512]{0:T(512)S(1)} %get-tuple-element.38), channel_id=1, replica_groups=mesh['groups'=2,'seq'=8,'chan'=2] {'seq'}, use_global_device_ids=true, to_apply=%region_7.8 | all-reduce | flops 11264 | bytes 90112 | tf_op jit(solution)/shard_map/psum | solution.py:187
  232.1 3.1 %collective-permute-done.17 = f32[3,3,512]{2,1,0:T(4,128)S(1)} collective-permute-done((f32[3,3,512]{2,1,0:T(4,128)S(1)}, f32[3,3,512]{2,1,0:T(4,128)S(1)}, u32[]{:S(2)}, u32[]{:S(2)}) %collective-permute-start.17) | collective-permute-done | bytes 18464 | tf_op jit(solution)/shard_map/ppermute | solution.py:32
  (146 shorter events, 58.5 us)
Async XLA Ops:
  0.6 6.8 %copy-start.5 = (f32[3,7,512]{2,1,0:T(8,128)S(1)}, f32[3,7,512]{2,1,0:T(8,128)}, u32[]{:S(2)}) copy-start(f32[3,7,512]{2,1,0:T(8,128)} %param.7) | copy-start | bytes 129028
  1.4 7.4 %collective-permute-start.1 = (bf16[3,3,512]{2,1,0:T(4,128)(2,1)S(1)}, bf16[3,3,512]{2,1,0:T(4,128)(2,1)S(1)}, u32[]{:S(2)}, u32[]{:S(2)}) collective-permute-start(bf16[3,3,512]{2,1,0:T(4,128)(2,1)S(1)} %get-tuple-element.58), channel_id=1, source_target_pairs={{2,0},{4,2},{6,4},{8,6},{10,8},{12,10},{14,12},{0,14},{3,1},{5,3},... | collective-permute-start | bytes 27656 | tf_op jit(solution)/shard_map/ppermute | solution.py:35
  7.5 6.4 %collective-permute-start = (bf16[3,3,512]{2,1,0:T(4,128)(2,1)S(1)}, bf16[3,3,512]{2,1,0:T(4,128)(2,1)S(1)}, u32[]{:S(2)}, u32[]{:S(2)}) collective-permute-start(bf16[3,3,512]{2,1,0:T(4,128)(2,1)S(1)} %get-tuple-element.59), channel_id=1, source_target_pairs={{0,2},{2,4},{4,6},{6,8},{8,10},{10,12},{12,14},{14,0},{1,3},{3,5},... | collective-permute-start | bytes 27656 | tf_op jit(solution)/shard_map/ppermute | solution.py:32
  7.5 6.3 %copy-start = (bf16[3,128,512]{2,1,0:T(8,128)(2,1)S(1)}, bf16[3,128,512]{2,1,0:T(8,128)(2,1)}, u32[]{:S(2)}) copy-start(bf16[3,128,512]{2,1,0:T(8,128)(2,1)} %param.5) | copy-start | bytes 1179652
  15.8 11.6 %all-to-all-start.5 = ((f32[1,1,128,512]{3,1,0,2:T(1,128)}), f32[1,1,128,512]{3,1,0,2:T(1,128)S(1)}, u32[]{:S(2)}, u32[]{:S(2)}) async-start(f32[1,1,128,512]{3,1,0,2:T(1,128)} %copy.54), calls=%async_computation.5 | async-start | bytes 524288 | tf_op jit(solution)/shard_map/all_to_all | solution.py:103
  27.3 16.0 %all-to-all-start = ((f32[2,1,128,512]{3,0,1,2:T(2,128)}), f32[2,1,128,512]{3,0,1,2:T(2,128)S(1)}, u32[]{:S(2)}, u32[]{:S(2)}) async-start(f32[2,1,128,512]{3,0,1,2:T(2,128)} %copy.38), calls=%async_computation | async-start | bytes 1048576 | tf_op jit(solution)/shard_map/all_to_all | solution.py:103
  43.4 11.9 %all-to-all-start.6 = ((f32[1,8,16,512]{3,2,0,1:T(8,128)}), f32[1,8,16,512]{3,2,0,1:T(8,128)S(1)}, u32[]{:S(2)}, u32[]{:S(2)}) async-start(f32[1,8,16,512]{3,2,0,1:T(8,128)} %copy.57), calls=%async_computation.6 | async-start | bytes 524288 | tf_op jit(solution)/shard_map/all_to_all | solution.py:107
  55.3 11.6 %all-to-all-start.7 = ((f32[1,8,16,512]{3,2,0,1:T(8,128)}), f32[1,8,16,512]{3,2,0,1:T(8,128)S(1)}, u32[]{:S(2)}, u32[]{:S(2)}) async-start(f32[1,8,16,512]{3,2,0,1:T(8,128)} %copy.58), calls=%async_computation.7 | async-start | bytes 524288 | tf_op jit(solution)/shard_map/all_to_all | solution.py:108
  66.9 17.4 %all-to-all-start.2 = ((f32[2,8,16,512]{3,2,0,1:T(8,128)}), f32[2,8,16,512]{3,2,0,1:T(8,128)S(1)}, u32[]{:S(2)}, u32[]{:S(2)}) async-start(f32[2,8,16,512]{3,2,0,1:T(8,128)} %copy.45), calls=%async_computation.2 | async-start | bytes 1048576 | tf_op jit(solution)/shard_map/all_to_all | solution.py:108
  84.3 17.9 %all-to-all-start.1 = ((f32[2,8,16,512]{3,2,0,1:T(8,128)}), f32[2,8,16,512]{3,2,0,1:T(8,128)S(1)}, u32[]{:S(2)}, u32[]{:S(2)}) async-start(f32[2,8,16,512]{3,2,0,1:T(8,128)} %copy.42), calls=%async_computation.1 | async-start | bytes 1048576 | tf_op jit(solution)/shard_map/all_to_all | solution.py:107
  104.5 1.2 copy-start.1
  113.1 30.9 %all-to-all-start.8 = ((f32[2,1,128,512]{3,0,1,2:T(2,128)}), f32[2,1,128,512]{3,0,1,2:T(2,128)}, u32[]{:S(2)}, u32[]{:S(2)}) async-start(f32[2,1,128,512]{3,0,1,2:T(2,128)} %copy.61), calls=%async_computation.8 | async-start | bytes 1048576 | tf_op jit(solution)/shard_map/all_to_all | solution.py:119
  119.2 12.0 %collective-permute-start.9 = (f32[2,1,16,512]{3,1,2,0:T(1,128)}, f32[2,1,16,512]{3,1,2,0:T(1,128)S(1)}, u32[]{:S(2)}, u32[]{:S(2)}) collective-permute-start(f32[2,1,16,512]{3,1,2,0:T(1,128)} %reshape_bitcast_fusion.6), channel_id=1, source_target_pairs={{0,2},{2,0},{4,6},{6,4},{8,10},{10,8},{12,14},{14,12},{1,3},{3,1},... | collective-permute-start | bytes 196616 | tf_op jit(solution)/shard_map/ppermute | solution.py:21
  121.5 13.1 %collective-permute-start.10 = (f32[2,1,16,512]{3,1,2,0:T(1,128)}, f32[2,1,16,512]{3,1,2,0:T(1,128)}, u32[]{:S(2)}, u32[]{:S(2)}) collective-permute-start(f32[2,1,16,512]{3,1,2,0:T(1,128)} %reshape_bitcast_fusion.5), channel_id=1, source_target_pairs={{0,4},{2,6},{4,0},{6,2},{8,12},{10,14},{12,8},{14,10},{1,5},{3,7},... | collective-permute-start | bytes 196616 | tf_op jit(solution)/shard_map/ppermute | solution.py:21
  123.7 13.1 %collective-permute-start.11 = (f32[2,1,16,512]{3,1,2,0:T(1,128)}, f32[2,1,16,512]{3,1,2,0:T(1,128)S(1)}, u32[]{:S(2)}, u32[]{:S(2)}) collective-permute-start(f32[2,1,16,512]{3,1,2,0:T(1,128)} %reshape_bitcast_fusion.4), channel_id=1, source_target_pairs={{0,6},{2,4},{4,2},{6,0},{8,14},{10,12},{12,10},{14,8},{1,7},{3,5},... | collective-permute-start | bytes 196616 | tf_op jit(solution)/shard_map/ppermute | solution.py:21
  124.1 15.3 %collective-permute-start.12 = (f32[2,1,16,512]{3,1,2,0:T(1,128)S(1)}, f32[2,1,16,512]{3,1,2,0:T(1,128)S(1)}, u32[]{:S(2)}, u32[]{:S(2)}) collective-permute-start(f32[2,1,16,512]{3,1,2,0:T(1,128)S(1)} %reshape_bitcast_fusion.3), channel_id=1, source_target_pairs={{0,8},{2,10},{4,12},{6,14},{8,0},{10,2},{12,4},{14,6},{1,9},{3,11}... | collective-permute-start | bytes 196616 | tf_op jit(solution)/shard_map/ppermute | solution.py:21
  126.8 15.0 %collective-permute-start.13 = (f32[2,1,16,512]{3,1,2,0:T(1,128)S(1)}, f32[2,1,16,512]{3,1,2,0:T(1,128)S(1)}, u32[]{:S(2)}, u32[]{:S(2)}) collective-permute-start(f32[2,1,16,512]{3,1,2,0:T(1,128)S(1)} %reshape_bitcast_fusion.2), channel_id=1, source_target_pairs={{0,10},{2,8},{4,14},{6,12},{8,2},{10,0},{12,6},{14,4},{1,11},{3,9}... | collective-permute-start | bytes 196616 | tf_op jit(solution)/shard_map/ppermute | solution.py:21
  131.2 11.6 %collective-permute-start.14 = (f32[2,1,16,512]{3,1,2,0:T(1,128)S(1)}, f32[2,1,16,512]{3,1,2,0:T(1,128)S(1)}, u32[]{:S(2)}, u32[]{:S(2)}) collective-permute-start(f32[2,1,16,512]{3,1,2,0:T(1,128)S(1)} %reshape_bitcast_fusion.1), channel_id=1, source_target_pairs={{0,12},{2,14},{4,8},{6,10},{8,4},{10,6},{12,0},{14,2},{1,13},{3,15... | collective-permute-start | bytes 196616 | tf_op jit(solution)/shard_map/ppermute | solution.py:21
  134.6 8.8 %collective-permute-start.15 = (f32[2,1,16,512]{3,1,2,0:T(1,128)S(1)}, f32[2,1,16,512]{3,1,2,0:T(1,128)S(1)}, u32[]{:S(2)}, u32[]{:S(2)}) collective-permute-start(f32[2,1,16,512]{3,1,2,0:T(1,128)S(1)} %reshape_bitcast_fusion), channel_id=1, source_target_pairs={{0,14},{2,12},{4,10},{6,8},{8,6},{10,4},{12,2},{14,0},{1,15},{3,13... | collective-permute-start | bytes 196616 | tf_op jit(solution)/shard_map/ppermute | solution.py:21
  136.8 28.4 %collective-permute-start.2 = (f32[1,1,16,512]{3,1,2,0:T(1,128)S(1)}, f32[1,1,16,512]{3,1,2,0:T(1,128)S(1)}, u32[]{:S(2)}, u32[]{:S(2)}) collective-permute-start(f32[1,1,16,512]{3,1,2,0:T(1,128)S(1)} %reshape_bitcast_fusion.14), channel_id=1, source_target_pairs={{0,2},{2,0},{4,6},{6,4},{8,10},{10,8},{12,14},{14,12},{1,3},{3,1},... | collective-permute-start | bytes 98312 | tf_op jit(solution)/shard_map/ppermute | solution.py:21
  139.3 29.3 %collective-permute-start.3 = (f32[1,1,16,512]{3,1,2,0:T(1,128)S(1)}, f32[1,1,16,512]{3,1,2,0:T(1,128)S(1)}, u32[]{:S(2)}, u32[]{:S(2)}) collective-permute-start(f32[1,1,16,512]{3,1,2,0:T(1,128)S(1)} %reshape_bitcast_fusion.13), channel_id=1, source_target_pairs={{0,4},{2,6},{4,0},{6,2},{8,12},{10,14},{12,8},{14,10},{1,5},{3,7},... | collective-permute-start | bytes 98312 | tf_op jit(solution)/shard_map/ppermute | solution.py:21
  141.8 27.4 %collective-permute-start.4 = (f32[1,1,16,512]{3,1,2,0:T(1,128)S(1)}, f32[1,1,16,512]{3,1,2,0:T(1,128)S(1)}, u32[]{:S(2)}, u32[]{:S(2)}) collective-permute-start(f32[1,1,16,512]{3,1,2,0:T(1,128)S(1)} %reshape_bitcast_fusion.12), channel_id=1, source_target_pairs={{0,6},{2,4},{4,2},{6,0},{8,14},{10,12},{12,10},{14,8},{1,7},{3,5},... | collective-permute-start | bytes 98312 | tf_op jit(solution)/shard_map/ppermute | solution.py:21
  144.0 13.2 %all-to-all-start.3 = ((f32[1,1,128,512]{3,1,0,2:T(1,128)}), f32[1,1,128,512]{3,1,0,2:T(1,128)S(1)}, u32[]{:S(2)}, u32[]{:S(2)}) async-start(f32[1,1,128,512]{3,1,0,2:T(1,128)} %copy.50), calls=%async_computation.3 | async-start | bytes 524288 | tf_op jit(solution)/shard_map/all_to_all | solution.py:119
  157.2 21.7 %all-to-all-start.9 = ((f32[2,8,16,512]{3,2,0,1:T(8,128)}), f32[2,8,16,512]{3,2,0,1:T(8,128)S(1)}, u32[]{:S(2)}, u32[]{:S(2)}) async-start(f32[2,8,16,512]{3,2,0,1:T(8,128)} %copy.65), calls=%async_computation.9 | async-start | bytes 1048576 | tf_op jit(solution)/shard_map/all_to_all | solution.py:125
  160.7 14.4 %collective-permute-start.5 = (f32[1,1,16,512]{3,1,2,0:T(1,128)S(1)}, f32[1,1,16,512]{3,1,2,0:T(1,128)S(1)}, u32[]{:S(2)}, u32[]{:S(2)}) collective-permute-start(f32[1,1,16,512]{3,1,2,0:T(1,128)S(1)} %reshape_bitcast_fusion.11), channel_id=1, source_target_pairs={{0,8},{2,10},{4,12},{6,14},{8,0},{10,2},{12,4},{14,6},{1,9},{3,11}... | collective-permute-start | bytes 98312 | tf_op jit(solution)/shard_map/ppermute | solution.py:21
  163.7 12.7 %collective-permute-start.6 = (f32[1,1,16,512]{3,1,2,0:T(1,128)S(1)}, f32[1,1,16,512]{3,1,2,0:T(1,128)S(1)}, u32[]{:S(2)}, u32[]{:S(2)}) collective-permute-start(f32[1,1,16,512]{3,1,2,0:T(1,128)S(1)} %reshape_bitcast_fusion.10), channel_id=1, source_target_pairs={{0,10},{2,8},{4,14},{6,12},{8,2},{10,0},{12,6},{14,4},{1,11},{3,9}... | collective-permute-start | bytes 98312 | tf_op jit(solution)/shard_map/ppermute | solution.py:21
  165.2 11.3 %collective-permute-start.7 = (f32[1,1,16,512]{3,1,2,0:T(1,128)S(1)}, f32[1,1,16,512]{3,1,2,0:T(1,128)S(1)}, u32[]{:S(2)}, u32[]{:S(2)}) collective-permute-start(f32[1,1,16,512]{3,1,2,0:T(1,128)S(1)} %reshape_bitcast_fusion.9), channel_id=1, source_target_pairs={{0,12},{2,14},{4,8},{6,10},{8,4},{10,6},{12,0},{14,2},{1,13},{3,15... | collective-permute-start | bytes 98312 | tf_op jit(solution)/shard_map/ppermute | solution.py:21
  168.6 8.1 %collective-permute-start.8 = (f32[1,1,16,512]{3,1,2,0:T(1,128)S(1)}, f32[1,1,16,512]{3,1,2,0:T(1,128)S(1)}, u32[]{:S(2)}, u32[]{:S(2)}) collective-permute-start(f32[1,1,16,512]{3,1,2,0:T(1,128)S(1)} %reshape_bitcast_fusion.8), channel_id=1, source_target_pairs={{0,14},{2,12},{4,10},{6,8},{8,6},{10,4},{12,2},{14,0},{1,15},{3,13... | collective-permute-start | bytes 98312 | tf_op jit(solution)/shard_map/ppermute | solution.py:21
  178.9 11.6 %all-to-all-start.4 = ((f32[1,8,16,512]{3,2,0,1:T(8,128)}), f32[1,8,16,512]{3,2,0,1:T(8,128)S(1)}, u32[]{:S(2)}, u32[]{:S(2)}) async-start(f32[1,8,16,512]{3,2,0,1:T(8,128)} %copy.53), calls=%async_computation.4 | async-start | bytes 524288 | tf_op jit(solution)/shard_map/all_to_all | solution.py:125
  182.6 7.9 %copy-start.6 = (f32[512]{0:T(512)S(1)}, f32[512]{0:T(512)}, u32[]{:S(2)}) copy-start(f32[512]{0:T(512)} %param.8) | copy-start | bytes 6148
  228.1 4.0 %collective-permute-start.16 = (f32[3,3,512]{2,1,0:T(4,128)S(1)}, f32[3,3,512]{2,1,0:T(4,128)S(1)}, u32[]{:S(2)}, u32[]{:S(2)}) collective-permute-start(f32[3,3,512]{2,1,0:T(4,128)S(1)} %get-tuple-element.46), channel_id=1, source_target_pairs={{2,0},{4,2},{6,4},{8,6},{10,8},{12,10},{14,12},{0,14},{3,1},{5,3},... | collective-permute-start | bytes 55304 | tf_op jit(solution)/shard_map/ppermute | solution.py:35
  228.6 6.5 %collective-permute-start.17 = (f32[3,3,512]{2,1,0:T(4,128)S(1)}, f32[3,3,512]{2,1,0:T(4,128)S(1)}, u32[]{:S(2)}, u32[]{:S(2)}) collective-permute-start(f32[3,3,512]{2,1,0:T(4,128)S(1)} %get-tuple-element.47), channel_id=1, source_target_pairs={{0,2},{2,4},{4,6},{6,8},{8,10},{10,12},{12,14},{14,0},{1,3},{3,5},... | collective-permute-start | bytes 55304 | tf_op jit(solution)/shard_map/ppermute | solution.py:32
  (3 other events, 3.0 us)
